TPU v7x, 256 devices: a whole 4x4x8 slice. The times are simulated.
256 devices in a mesh: seq: 8 (over x, core), exp: 32 (over y, z).
Axes of the slice: x: 4, y: 4, z: 8, core: 2. Of those that a mesh axis runs over, the one named last changes fastest.
Arguments:
- tokens: bfloat16 [4096, 7168], P('exp', 'seq'), may hold values from -6 to 6
- out_grad: bfloat16 [4096, 7168], P('exp', 'seq'), may hold values from -6 to 6
- expert_ids: int32 [4096, 8], P('exp'), may hold values from 0 to 255, as said below
- route_weights: float32 [4096, 8], P('exp'), may hold values from 0.2 to 2.5
- gate_proj: bfloat16 [32, 7168, 2048], P('exp', None, 'seq'), may hold values from -0.0625 to 0.0625
- up_proj: bfloat16 [32, 7168, 2048], P('exp', None, 'seq'), may hold values from -0.0625 to 0.0625
- down_proj: bfloat16 [32, 2048, 7168], P('exp', 'seq'), may hold values from -0.125 to 0.125
Outputs:
- token_grad: bfloat16 [4096, 7168], P('exp', 'seq')
- route_grad: float32 [4096, 8], P('exp', 'seq')
Inputs may be any that keep to these rules, and one draw needn't show every extreme that they name: `expert_ids`: each row names 8 different experts, at most one of them below 32; between 96 and all of the 128 rows of one index of exp name one below 32; those rows name any one expert below 32 at most 8 times, and in every draw one such expert exactly 8 times on every index of exp.
All inputs are finite; a program needn't handle non-finite values.
Results may differ from a plain program's by a relative error of at most 0.0049.
Values may be sent and summed in bfloat16 or wider, within the bound.
A program may use at most 128 MiB of HBM per device.

v0:
```python
import jax
import jax.numpy as jnp
from jax import lax
from jax.sharding import PartitionSpec as P

PRECISE = lax.Precision.HIGHEST
CONTRACT = (((1,), (1,)), ((), ()))


def expert_front(row_inputs, row_grads, w_gate, w_up, w_down):
    pre_gate = jnp.dot(row_inputs, w_gate, preferred_element_type=jnp.float32)
    pre_up = jnp.dot(row_inputs, w_up, preferred_element_type=jnp.float32)
    back_grad = lax.dot_general(row_grads, w_down, CONTRACT, preferred_element_type=jnp.float32)
    gate_sig = jax.nn.sigmoid(pre_gate)
    active = pre_gate * gate_sig
    route_part = jnp.sum(active * pre_up * back_grad, axis=-1)
    grad_gate = (back_grad * pre_up * gate_sig * (1.0 + pre_gate * (1.0 - gate_sig))).astype(
        jnp.bfloat16
    )
    grad_up = (back_grad * active).astype(jnp.bfloat16)
    return (grad_gate, grad_up, route_part)


def expert_back(grad_gate, grad_up, w_gate, w_up):
    return lax.dot_general(
        grad_gate, w_gate, CONTRACT, preferred_element_type=jnp.float32
    ) + lax.dot_general(grad_up, w_up, CONTRACT, preferred_element_type=jnp.float32)


def slot_match(route_ids, most_rows, slot_count):
    expert_total = slot_count // most_rows
    named_hot = (route_ids[..., None] == jnp.arange(expert_total, dtype=jnp.int32)).astype(
        jnp.int32
    )
    per_token = jnp.sum(named_hot, axis=1)
    earlier = jnp.cumsum(per_token, axis=0) - per_token
    slot_rank = jnp.sum(named_hot * earlier[:, None, :], axis=-1)
    target = route_ids * most_rows + slot_rank
    return target[..., None] == jnp.arange(slot_count, dtype=jnp.int32)


def local(tokens, out_grad, expert_ids, route_weights, gate_proj, up_proj, down_proj):
    exp_count = lax.axis_size("exp")
    tok_dev = tokens.shape[0]
    expert_count = exp_count * gate_proj.shape[0]
    most_rows = max(2, 2 * ((tok_dev + expert_count - 1) // expert_count))
    slot_count = expert_count * most_rows
    w_gate = gate_proj[0]
    w_up = up_proj[0]
    w_down = down_proj[0]
    full_x, full_dy = (
        lax.all_gather(tokens, "seq", axis=1, tiled=True),
        lax.all_gather(out_grad, "seq", axis=1, tiled=True),
    )
    model_width = full_x.shape[1]
    matched = slot_match(expert_ids, most_rows, slot_count)
    selector = jnp.sum(matched, axis=1).astype(jnp.bfloat16)
    both_rows = jnp.concatenate([full_x, full_dy], axis=1)
    packed = jnp.einsum(
        "ts,td->sd", selector, both_rows, preferred_element_type=jnp.float32
    ).astype(jnp.bfloat16)
    packed = packed.reshape(expert_count, most_rows, 2 * model_width)
    weighted = jnp.sum(jnp.where(matched, route_weights[..., None], 0.0), axis=1)
    matched_float = matched.astype(jnp.float32)
    arrived = lax.all_to_all(packed, "exp", split_axis=0, concat_axis=0, tiled=True)
    layout = arrived.shape
    flat_rows = arrived.reshape(-1, layout[2])
    grad_gate, grad_up, route_part = expert_front(
        flat_rows[:, :model_width], flat_rows[:, model_width:], w_gate, w_up, w_down
    )
    slot_grad = expert_back(grad_gate, grad_up, w_gate, w_up).reshape(
        layout[0], layout[1], model_width
    )
    back_grad = lax.all_to_all(slot_grad, "exp", split_axis=0, concat_axis=0, tiled=True)
    back_route = lax.all_to_all(
        route_part.reshape(layout[0], layout[1]), "exp", split_axis=0, concat_axis=0, tiled=True
    )
    token_part = jnp.dot(weighted, back_grad.reshape(slot_count, model_width), precision=PRECISE)
    route_part = jnp.einsum(
        "tks,s->tk", matched_float, back_route.reshape(slot_count), precision=PRECISE
    )
    own_grad, own_route = (
        lax.psum_scatter(token_part, "seq", scatter_dimension=1, tiled=True),
        lax.psum_scatter(route_part, "seq", scatter_dimension=1, tiled=True),
    )
    return (own_grad.astype(jnp.bfloat16), own_route)


def solution(mesh):
    in_specs = (
        P("exp", "seq"),
        P("exp", "seq"),
        P("exp", None),
        P("exp", None),
        P("exp", None, "seq"),
        P("exp", None, "seq"),
        P("exp", "seq", None),
    )
    out_specs = (P("exp", "seq"), P("exp", "seq"))
    return jax.shard_map(local, mesh=mesh, in_specs=in_specs, out_specs=out_specs, check_vma=False)
```

profile of v0, /device:TPU:1, one launch (start us, length us, event | category | flops | bytes accessed | tf_op | source)
XLA Modules:
  0.0 482.6 jit_solution(10725312584192944092)
XLA Ops:
  7.2 0.7 all-gather.3.cloned.1.call-update
  7.9 0.7 all-gather.5.cloned.1.call-update
  8.6 0.7 convert_reduce_fusion.1
  9.7 0.7 select_reduce_fusion.1
  10.4 0.7 multiply_add_fusion
  11.2 0.4 convert_reduce_fusion
  11.6 29.9 %all-gather.3.cloned.1.call-done = bf16[128,7168]{1,0:T(8,128)(2,1)} async-done(((bf16[128,896]{1,0:T(8,128)(2,1)}), bf16[128,7168]{1,0:T(8,128)(2,1)}) %all-gather.3.cloned.1.call-update) | async-done | bytes 1835024 | tf_op jit(solution)/shard_map/all_gather | solution.py:52
  41.5 29.5 %all-gather.5.cloned.1.call-done = bf16[128,7168]{1,0:T(8,128)(2,1)} async-done(((bf16[128,896]{1,0:T(8,128)(2,1)}), bf16[128,7168]{1,0:T(8,128)(2,1)}) %all-gather.5.cloned.1.call-update) | async-done | bytes 1835024 | tf_op jit(solution)/shard_map/all_gather | solution.py:53
  71.0 4.1 fusion
  75.2 169.6 %all_to_all.19 = bf16[32,8,14336]{2,1,0:T(8,128)(2,1)S(1)} all-to-all(bf16[32,8,14336]{2,1,0:T(8,128)(2,1)S(1)} %fusion), channel_id=1, replica_groups=mesh['seq'=8,'exp'=32] {'exp'}, dimensions={0} | all-to-all | bytes 14680064 | tf_op jit(solution)/shard_map/all_to_all | solution.py:65
  244.8 1.6 fusion.11
  246.4 0.4 copy-done
  246.8 1.6 fusion.14
  248.4 0.4 copy-done.3
  248.9 1.2 multiply_reduce_fusion
  250.0 1.2 fusion.9
  251.3 4.2 fusion.1
  255.5 8.3 %all-to-all-start.1 = ((f32[32,8,7168]{2,1,0:T(8,128)}), f32[32,8,7168]{2,1,0:T(8,128)}, u32[]{:S(2)}, u32[]{:S(2)}) async-start(f32[32,8,7168]{2,1,0:T(8,128)} %fusion.1), calls=%async_computation.1 | async-start | bytes 14680064 | tf_op jit(solution)/shard_map/all_to_all | solution.py:74
  263.8 0.2 reduce-scatter.2.cloned.1.call-start
  264.2 0.4 select_reduce_fusion
  264.6 160.2 %all-to-all-done.1 = f32[32,8,7168]{2,1,0:T(8,128)} async-done(((f32[32,8,7168]{2,1,0:T(8,128)}), f32[32,8,7168]{2,1,0:T(8,128)}, u32[]{:S(2)}, u32[]{:S(2)}) %all-to-all-start.1) | async-done | bytes 7340064 | tf_op jit(solution)/shard_map/all_to_all | solution.py:74
  424.8 9.1 %fusion.2 = f32[128,7168]{1,0:T(8,128)} fusion(f32[128,256]{1,0:T(8,128)S(1)} %select_reduce_fusion, f32[32,8,7168]{2,1,0:T(8,128)} %all-to-all-done.1), kind=kOutput, calls=%fused_computation.4 | convolution fusion | flops 2818572288 | bytes 11141120 | tf_op jit(solution)/shard_map/dot_general | solution.py:78
  434.0 0.7 all_to_all.14
  434.6 10.8 %all-to-all-start.2 = ((f32[32,1,8]{2,1,0:T(1,128)}), f32[32,1,8]{2,1,0:T(1,128)S(1)}, u32[]{:S(2)}, u32[]{:S(2)}) async-start(f32[32,1,8]{2,1,0:T(1,128)} %bitcast.7), calls=%async_computation.3 | async-start | bytes 32768 | tf_op jit(solution)/shard_map/all_to_all | solution.py:75
  445.4 0.6 dynamic-slice
  446.1 7.9 %all-to-all-done.2 = f32[32,1,8]{2,1,0:T(1,128)S(1)} async-done(((f32[32,1,8]{2,1,0:T(1,128)}), f32[32,1,8]{2,1,0:T(1,128)S(1)}, u32[]{:S(2)}, u32[]{:S(2)}) %all-to-all-start.2) | async-done | bytes 1056 | tf_op jit(solution)/shard_map/all_to_all | solution.py:75
  454.0 0.5 broadcast.25
  454.5 0.7 reduce.3
  455.3 3.6 fusion.19
  459.0 14.1 %all-reduce = f32[128,8]{0,1:T(8,128)S(1)} all-reduce(f32[128,8]{0,1:T(8,128)S(1)} %bitcast.31), channel_id=3, replica_groups=mesh['seq'=8,'exp'=32] {'seq'}, use_global_device_ids=true, to_apply=%region_7.8.clone | all-reduce | flops 1024 | bytes 8192
  473.1 1.2 constant_dynamic-slice_fusion
  474.3 1.7 convert_element_type.28
  (20 shorter events, 0.8 us)
Async XLA Ops:
  7.2 34.3 %all-gather.3.cloned.1.call-start = ((), (), s32[]{:S(2)}) async-start(), calls=%async_computation.4 | async-start | bytes 2064384 | tf_op jit(solution)/shard_map/all_gather | solution.py:52
  7.9 63.1 %all-gather.5.cloned.1.call-start = ((), (), s32[]{:S(2)}) async-start(), calls=%async_computation.5 | async-start | bytes 2064384 | tf_op jit(solution)/shard_map/all_gather | solution.py:53
  75.2 169.6 %copy-start.1 = (bf16[1,7168,256]{2,1,0:T(8,128)(2,1)S(1)}, bf16[1,7168,256]{2,1,0:T(8,128)(2,1)}, u32[]{:S(2)}) copy-start(bf16[1,7168,256]{2,1,0:T(8,128)(2,1)} %param.11) | copy-start | bytes 11010052
  244.8 2.0 copy-start
  246.8 2.0 copy-start.3
  255.5 8.6 %copy-start.2 = (f32[128,8]{0,1:T(8,128)S(1)}, f32[128,8]{0,1:T(8,128)}, u32[]{:S(2)}) copy-start(f32[128,8]{0,1:T(8,128)} %param.10) | copy-start | bytes 12292
  255.5 169.3 %all-to-all-start.1 = ((f32[32,8,7168]{2,1,0:T(8,128)}), f32[32,8,7168]{2,1,0:T(8,128)}, u32[]{:S(2)}, u32[]{:S(2)}) async-start(f32[32,8,7168]{2,1,0:T(8,128)} %fusion.1), calls=%async_computation.1 | async-start | bytes 14680064 | tf_op jit(solution)/shard_map/all_to_all | solution.py:74
  263.8 210.5 %reduce-scatter.2.cloned.1.call-start = ((), (), s32[]{:S(2)}) async-start(), calls=%async_computation.6 | async-start | bytes 4128768 | tf_op jit(solution)/shard_map/reduce_scatter | solution.py:83
  433.9 11.5 %copy-start.4 = (u32[256]{0:T(256)S(1)}, u32[256]{0:T(256)}, u32[]{:S(2)}) copy-start(u32[256]{0:T(256)} %constant.17) | copy-start | bytes 3076
  434.6 19.4 %all-to-all-start.2 = ((f32[32,1,8]{2,1,0:T(1,128)}), f32[32,1,8]{2,1,0:T(1,128)S(1)}, u32[]{:S(2)}, u32[]{:S(2)}) async-start(f32[32,1,8]{2,1,0:T(1,128)} %bitcast.7), calls=%async_computation.3 | async-start | bytes 32768 | tf_op jit(solution)/shard_map/all_to_all | solution.py:75
Sparse Core Ops, SparseCore 0:
  9.8 31.6 all-gather.2
  43.3 27.6 all-gather.4
  434.1 38.8 reduce-scatter.1
where the time goes:
time: 483 us
  waiting for transfers between devices  229 us (47%)
  blocking collectives  184 us (38%)
  matrix products  26.7 us (6%)
  starting transfers between devices  19.4 us (4%)
  between operations  13.9 us (3%)
  other arithmetic  5.49 us (1%)
    all_to_all x1, blocking collectives, local(): lax.all_to_all(packed, 'exp', split_axis=0, concat_axis=0, tiled=True)  170 us
    all_to_all x1, waiting for transfers between devices, local(): lax.all_to_all(slot_grad, 'exp', split_axis=0, concat_axis=0, tiled=True)  160 us
    all_gather x1, waiting for transfers between devices, local(): lax.all_gather(tokens, 'seq', axis=1, tiled=True)  29.9 us
    all_gather x1, waiting for transfers between devices, local(): lax.all_gather(out_grad, 'seq', axis=1, tiled=True)  29.5 us
    unnamed x1, blocking collectives  14.1 us
    all_to_all x1, starting transfers between devices, local(): lax.all_to_all(route_part.reshape(layout[0], layout[1]), 'exp', split_axi...  10.8 us
  transfers between devices with their start and end apart: 5, of which 4 were waited for; matrix products, arithmetic and copies ran while one was open for 2% of the time, Pallas kernels for 0%

commit v1 on v0

v1 whole, which is shorter than its diff:
```python
import jax
import jax.numpy as jnp
from jax import lax
from jax.experimental import pallas as pl
from jax.experimental.pallas import tpu as pltpu
from jax.sharding import PartitionSpec as P

MESH = pl.DeviceIdType.MESH
BF = jnp.bfloat16
F32 = jnp.float32
NX, NC, NY, NZ = 4, 2, 4, 8
NE = NY * NZ
MOST = 8
SLOTS = NE * MOST
CHUNKS = 4
PER = NE // CHUNKS
NT = (((1,), (1,)), ((), ()))
TN = (((0,), (0,)), ((), ()))


def z_step(index):
    half = (index + 1) // 2
    return (NZ + half * (2 * (index % 2) - 1)) % NZ


def kernel(tok, og, ids, rw, wg_h, wu_h, wd_h, tg_out, rg_out,
           wgu, wd, packed, xg, acc, gbuf, ps, pb, own, relay, snd, fin, rets, ret,
           selbuf, rpart, rtot, rret,
           wsem, disp_r, ag_r, far_r, core_r, pair_r, rel_r, fin_r, ret_r, rp_r, rr_r, send_s):
    seq, exp = lax.axis_index("seq"), lax.axis_index("exp")
    x, c = seq // NC, seq % NC
    y, z = exp // NZ, exp % NZ
    f = tok.shape[1]

    def at_x(step, flip=0):
        return {"seq": NC * ((x + step) % NX) + (c + flip) % NC}

    def to_exp(j):
        dz = z_step(j // NY)
        return {"exp": ((y + j % NY) % NY) * NZ + (z + dz) % NZ}

    def from_exp(j):
        dz = z_step(j // NY)
        return {"exp": ((y + NY - j % NY) % NY) * NZ + (z + NZ - dz) % NZ}

    def copy(src, dst, ssem, rsem, dev):
        return pltpu.make_async_remote_copy(
            src_ref=src, dst_ref=dst, send_sem=ssem, recv_sem=rsem,
            device_id=dev, device_id_type=MESH)

    def got(ref, sem):
        pltpu.make_async_copy(ref, ref, sem).wait()

    wcopies = []
    for k in range(NX * NC):
        dx, flip = k // NC, k % NC
        first = pl.multiple_of((NC * ((x + NX - dx) % NX) + (c + flip) % NC) * f, 128)
        h = wg_h.shape[1]
        for n, (src, dst) in enumerate((
                (wg_h.at[pl.ds(first, f), :], wgu.at[k, :, 0:h]),
                (wu_h.at[pl.ds(first, f), :], wgu.at[k, :, h:2 * h]),
                (wd_h.at[:, pl.ds(first, f)], wd.at[k]))):
            one = pltpu.make_async_copy(src, dst, wsem.at[k, n])
            one.start()
            wcopies.append(one)

    barrier = pltpu.get_barrier_semaphore()

    @pl.loop(1, NE)
    def _(j):
        pl.semaphore_signal(barrier, inc=1, device_id=to_exp(j), device_id_type=MESH)

    for k in range(1, NX * NC):
        pl.semaphore_signal(barrier, inc=1, device_id=at_x(k // NC, k % NC), device_id_type=MESH)

    q = lax.broadcasted_iota(jnp.int32, (SLOTS, tok.shape[0]), 0)
    j = q >> 3
    i = j >> 2
    half = (i + 1) >> 1
    dz = (NZ + half * (2 * (i & 1) - 1)) & (NZ - 1)
    wanted = ((y + (j & 3)) & 3) * NZ + ((z + dz) & 7)
    hot = ids[0:1, :] == wanted
    for k in range(1, ids.shape[0]):
        hot = hot | (ids[k:k + 1, :] == wanted)
    hot = jnp.where(hot, 1.0, 0.0)
    t0 = lax.broadcasted_iota(jnp.int32, (tok.shape[0], tok.shape[0]), 0)
    t1 = lax.broadcasted_iota(jnp.int32, (tok.shape[0], tok.shape[0]), 1)
    before = jnp.where(t0 < t1, 1.0, 0.0).astype(BF)
    rank = jnp.dot(hot.astype(BF), before, preferred_element_type=F32)
    sel = jnp.where(rank == (q & 7).astype(F32), hot, 0.0)
    selbuf[...] = sel
    selb = sel.astype(BF)
    for n, src in enumerate((tok, og)):
        rows = jnp.dot(selb, src[...], preferred_element_type=F32)
        rows = rows.reshape(NE, MOST, f).astype(BF)
        packed[:, :, n * f:(n + 1) * f] = rows
        xg[0, 0:1, :, n * f:(n + 1) * f] = rows[0:1]

    pl.semaphore_wait(barrier, NE - 1 + NX * NC - 1)

    @pl.loop(1, NE)
    def _(j):
        copy(packed.at[j], xg.at[0, j], send_s.at[0], disp_r.at[j // PER], to_exp(j)).start()

    def rows_of(r):
        return pl.ds(r * PER, PER)

    def own_chunk(r):
        lo = 1 if r == 0 else r * PER
        part = xg.at[0, lo:(r + 1) * PER]
        got(part, disp_r.at[r])
        mine = xg.at[0, rows_of(r)]
        copy(mine, xg.at[2, rows_of(r)], send_s.at[1], ag_r.at[0, r], at_x(1)).start()
        copy(mine, xg.at[6, rows_of(r)], send_s.at[2], ag_r.at[1, r], at_x(3)).start()
        copy(mine, xg.at[1, rows_of(r)], send_s.at[3], core_r.at[0], at_x(0, 1)).start()

    hp = PER // 2

    def near_chunk(r):
        for n, (slot, step) in enumerate(((2, 1), (6, 3))):
            part = xg.at[slot, rows_of(r)]
            got(part, ag_r.at[n, r])
            lo = r * PER + n * hp
            copy(xg.at[slot, lo:lo + hp], xg.at[4, lo:lo + hp], send_s.at[4 + n], far_r.at[n, r], at_x(step)).start()
            copy(part, xg.at[slot + 1, rows_of(r)], send_s.at[6 + n], core_r.at[slot // 2], at_x(0, 1)).start()

    def far_chunk(r):
        for n in range(2):
            lo = r * PER + n * hp
            got(xg.at[4, lo:lo + hp], far_r.at[n, r])
        copy(xg.at[4, rows_of(r)], xg.at[5, rows_of(r)], send_s.at[8], core_r.at[2], at_x(0, 1)).start()

    h2 = wgu.shape[2]

    def front(k, first=False):
        for n in range(3):
            wcopies[3 * k + n].wait()
        xs = xg[k, :, :, 0:f].reshape(SLOTS, f)
        ds = xg[k, :, :, f:2 * f].reshape(SLOTS, f)
        gu = jnp.dot(xs, wgu[k], preferred_element_type=F32)
        bg = lax.dot_general(ds, wd[k], NT, preferred_element_type=F32)
        if first:
            acc[:, 0:h2] = gu
            acc[:, h2:] = bg
        else:
            acc[:, 0:h2] += gu
            acc[:, h2:] += bg

    own_chunk(0)
    own_chunk(1)
    near_chunk(0)
    own_chunk(2)
    near_chunk(1)
    own_chunk(3)
    near_chunk(2)
    front(0, True)
    far_chunk(0)
    near_chunk(3)
    got(xg.at[1], core_r.at[0])
    front(1)
    far_chunk(1)
    far_chunk(2)
    front(2)
    front(6)
    far_chunk(3)
    got(xg.at[3], core_r.at[1])
    front(3)
    got(xg.at[7], core_r.at[3])
    front(7)
    front(4)
    got(xg.at[5], core_r.at[2])
    front(5)

    h = h2 // 2
    pre_g = acc[:, 0:h]
    pre_u = acc[:, h:h2]
    back = acc[:, h2:]
    sig = 1.0 / (1.0 + jnp.exp(-pre_g))
    active = pre_g * sig
    gbuf[:, 0:h] = (back * pre_u * sig * (1.0 + pre_g * (1.0 - sig))).astype(BF)
    gbuf[:, h:h2] = (back * active).astype(BF)
    prod = active * pre_u * back
    part = lax.dot_general(jnp.ones((8, h), F32), prod, NT, preferred_element_type=F32,
                           precision=lax.Precision.HIGHEST)
    rpart[0] = part[0:1, :]
    for k in range(1, NX * NC):
        copy(rpart.at[0], rpart.at[k], send_s.at[9], rp_r, at_x(k // NC, k % NC)).start()

    def product(d, flip):
        k = ((NX - d) % NX) * NC + flip
        return lax.dot_general(gbuf[...], wgu[k], NT, preferred_element_type=F32)

    def share(d):
        ps[d] = product(d, 1).astype(BF)
        copy(ps.at[d], pb.at[d], send_s.at[10], pair_r.at[d], at_x(0, 1)).start()
        own[d] = product(d, 0)

    def paired(d):
        got(pb.at[d], pair_r.at[d])
        own[d] += pb[d].astype(F32)

    m = SLOTS // 2
    halves = (slice(0, m), slice(m, SLOTS))
    share(2)
    share(1)
    paired(2)
    snd[0] = own[2].astype(BF)
    for n, step in enumerate((1, 3)):
        copy(snd.at[0, halves[n]], relay.at[n], send_s.at[11 + n], rel_r.at[n], at_x(step)).start()
    share(3)
    paired(1)
    snd[1, halves[1]] = own[1, halves[1]].astype(BF)
    copy(snd.at[1, halves[1]], fin.at[0, halves[1]], send_s.at[13], fin_r.at[0, 1], at_x(1)).start()
    share(0)
    paired(3)
    snd[2, halves[0]] = own[3, halves[0]].astype(BF)
    copy(snd.at[2, halves[0]], fin.at[1, halves[0]], send_s.at[14], fin_r.at[1, 0], at_x(3)).start()
    for n, (slot, d) in enumerate(((1, 1), (2, 3))):
        got(relay.at[n], rel_r.at[n])
        snd[slot, halves[n]] = (own[d, halves[n]] + relay[n].astype(F32)).astype(BF)
        copy(snd.at[slot, halves[n]], fin.at[n, halves[n]], send_s.at[15 + n], fin_r.at[n, n], at_x(d)).start()
    paired(0)

    got(rpart.at[1:8], rp_r)
    total = rpart[0]
    for k in range(1, NX * NC):
        total = total + rpart[k]
    rtot[...] = total
    rret[0] = total

    @pl.loop(1, NE)
    def _(j):
        copy(rtot, rret.at[j], send_s.at[17], rr_r, from_exp(j)).start()

    for n in range(2):
        got(fin.at[0, halves[n]], fin_r.at[0, n])
        got(fin.at[1, halves[n]], fin_r.at[1, n])
        s = own[0, halves[n]] + fin[0, halves[n]].astype(F32) + fin[1, halves[n]].astype(F32)
        s = s.reshape(NE // 2, MOST, f).astype(BF)
        rets[n * (NE // 2):(n + 1) * (NE // 2)] = s
        if n == 0:
            ret[0:1] = s[0:1]

        @pl.loop(max(1, n * (NE // 2)), (n + 1) * (NE // 2))
        def _(j):
            copy(rets.at[j], ret.at[j], send_s.at[18], ret_r, from_exp(j)).start()

    got(rret.at[1:NE], rr_r)
    lane = lax.broadcasted_iota(jnp.int32, (NE, 1, SLOTS), 2) >> 3
    row = lax.broadcasted_iota(jnp.int32, (NE, 1, SLOTS), 0)
    by_slot = jnp.sum(jnp.where(lane == row, rret[...], 0.0), axis=0)
    by_token = jnp.dot(jnp.broadcast_to(by_slot, (8, SLOTS)), selbuf[...], preferred_element_type=F32,
                       precision=lax.Precision.HIGHEST)
    rg_out[...] = jnp.where(ids[pl.ds(seq, 1), :] < NE, by_token[0:1, :], 0.0)

    weight = jnp.sum(jnp.where(ids[...] < NE, rw[...], 0.0), axis=0, keepdims=True)
    scale = jnp.sum(selbuf[...] * weight, axis=1, keepdims=True)
    got(ret.at[1:NE], ret_r)
    rows = (ret[...].reshape(SLOTS, f).astype(F32) * scale).astype(BF)
    tg_out[...] = lax.dot_general(selbuf[...].astype(BF), rows, TN, preferred_element_type=F32).astype(BF)

    got(packed.at[1:NE], send_s.at[0])
    for n in range(1, 4):
        got(xg.at[0], send_s.at[n])
    for n in range(2):
        got(xg.at[0, 0:NE // 2], send_s.at[4 + n])
        got(xg.at[0], send_s.at[6 + n])
    got(xg.at[0], send_s.at[8])
    got(rpart.at[1:8], send_s.at[9])
    got(ps, send_s.at[10])
    for n in range(2):
        got(relay.at[n], send_s.at[11 + n])
        got(relay.at[n], send_s.at[13 + n])
        got(relay.at[n], send_s.at[15 + n])
    got(rret.at[1:NE], send_s.at[17])
    got(rets.at[1:NE], send_s.at[18])


def local(tokens, out_grad, expert_ids, route_weights, gate_proj, up_proj, down_proj):
    t, f = tokens.shape
    h = gate_proj.shape[2]
    vmem = pl.BlockSpec(memory_space=pltpu.VMEM)
    anym = pl.BlockSpec(memory_space=pl.ANY)
    dma = pltpu.SemaphoreType.DMA
    token_grad, route_grad = pl.pallas_call(
        kernel,
        out_shape=(jax.ShapeDtypeStruct((t, f), BF), jax.ShapeDtypeStruct((1, t), F32)),
        in_specs=[vmem] * 4 + [anym] * 3,
        out_specs=(vmem, vmem),
        scratch_shapes=[
            pltpu.VMEM((8, f, 2 * h), BF),
            pltpu.VMEM((8, h, f), BF),
            pltpu.VMEM((NE, MOST, 2 * f), BF),
            pltpu.VMEM((8, NE, MOST, 2 * f), BF),
            pltpu.VMEM((SLOTS, 3 * h), F32),
            pltpu.VMEM((SLOTS, 2 * h), BF),
            pltpu.VMEM((4, SLOTS, f), BF),
            pltpu.VMEM((4, SLOTS, f), BF),
            pltpu.VMEM((4, SLOTS, f), F32),
            pltpu.VMEM((2, SLOTS // 2, f), BF),
            pltpu.VMEM((3, SLOTS, f), BF),
            pltpu.VMEM((2, SLOTS, f), BF),
            pltpu.VMEM((NE, MOST, f), BF),
            pltpu.VMEM((NE, MOST, f), BF),
            pltpu.VMEM((SLOTS, t), F32),
            pltpu.VMEM((8, 1, SLOTS), F32),
            pltpu.VMEM((1, SLOTS), F32),
            pltpu.VMEM((NE, 1, SLOTS), F32),
            dma((8, 3)), dma((CHUNKS,)), dma((2, CHUNKS)), dma((2, CHUNKS)), dma((4,)),
            dma((4,)), dma((2,)), dma((2, 2)), dma(()), dma(()), dma(()), dma((19,)),
        ],
        compiler_params=pltpu.CompilerParams(
            collective_id=0, has_side_effects=True, vmem_limit_bytes=60 * 1024 * 1024),
        name="moe_back",
    )(tokens, out_grad, expert_ids.T, route_weights.T, gate_proj[0], up_proj[0], down_proj[0])
    return token_grad, route_grad.reshape(t, 1)


def solution(mesh):
    in_specs = (
        P("exp", "seq"),
        P("exp", "seq"),
        P("exp", None),
        P("exp", None),
        P("exp", None, "seq"),
        P("exp", None, "seq"),
        P("exp", "seq", None),
    )
    out_specs = (P("exp", "seq"), P("exp", "seq"))
    return jax.shard_map(local, mesh=mesh, in_specs=in_specs, out_specs=out_specs, check_vma=False)
```

time: 483 us -> 95.3 us (0.20)
  waiting for transfers between devices: 229 us -> 0 us
  blocking collectives: 184 us -> 0 us
  Pallas kernels: 0 us -> 91.7 us
  matrix products: 26.7 us -> 0 us
  starting transfers between devices: 19.4 us -> 0 us
  between operations: 13.9 us -> 0.64 us
  other arithmetic: 5.49 us -> 0 us
    all_to_all x1 -> x0, blocking collectives: 170 us -> none  [local(): lax.all_to_all(packed, 'exp', split_axis=0, concat_axis=0, tiled=True)]
    all_to_all x2 -> x0, waiting for transfers between devices: 168 us -> none  [the longest x1 160 us: local(): lax.all_to_all(slot_grad, 'exp', split_axis=0, concat_axis=0, tiled=True)]
    pallas_call x0 -> x1, Pallas kernels: none -> 91.7 us  [local(): pl.pallas_call(kernel, out_shape=(jax.ShapeDtypeStruct((t, f), BF), jax.S...]
    all_gather x2 -> x0, waiting for transfers between devices: 59.4 us -> none  [the longest x1 29.9 us: local(): lax.all_gather(tokens, 'seq', axis=1, tiled=True)]
    dot_general x8 -> x0, matrix products: 26.7 us -> none  [the longest x1 9.12 us: local(): jnp.dot(weighted, back_grad.reshape(slot_count, model_width), precision=P...]
    all_to_all x2 -> x0, starting transfers between devices: 19.1 us -> none  [the longest x1 10.8 us: local(): lax.all_to_all(route_part.reshape(layout[0], layout[1]), 'exp', split_axi...]
    unnamed x1 -> x0, blocking collectives: 14.1 us -> none
  transfers between devices with their start and end apart: 5 -> 0, of which waited for: 4 -> 0; matrix products, arithmetic and copies ran while one was open for 2% -> 0% of each run, Pallas kernels for 0% -> 0%
where the time goes in v1:
time: 95.3 us; the launch traced here: 95.2 us
  Pallas kernels  91.7 us (96%)
  local copies, waits for them, and re-layouts  2.79 us (3%)
    pallas_call x1, Pallas kernels, local(): pl.pallas_call(kernel, out_shape=(jax.ShapeDtypeStruct((t, f), BF), jax.S...  91.7 us
    unnamed x2, local copies, waits for them, and re-layouts  2.79 us

profile of v1, /device:TPU:1, one launch (start us, length us, event | category | flops | bytes accessed | tf_op | source)
XLA Modules:
  0.0 95.2 jit_solution(8591861887645578140)
XLA Ops:
  0.6 91.7 %moe_back.1 = (bf16[128,896]{1,0:T(8,128)(2,1)}, f32[1,128]{1,0:T(1,128)}) custom-call(bf16[128,896]{1,0:T(8,128)(2,1)} %tok.1, bf16[128,896]{1,0:T(8,128)(2,1)} %og.1, s32[8,128]{1,0:T(8,128)} %bitcast.9, f32[8,128]{1,0:T(8,128)} %bitcast.10, bf16[7168,256]{1,0:T(8,128)(2,1)} %bitcast.6, bf16[7168,256]{1,0:T(8,128)(2,1)} %bitcast.7, bf16[256,7168]{1,0:T(8,128)(2,1)} %bitcast.8), custom_call_target="tpu_custom_call" | custom-call | tf_op jit(solution)/shard_map/moe_back/pallas_call | solution.py:285
  92.4 1.6 %copy.11 = bf16[128,896]{1,0:T(8,128)(2,1)} copy(bf16[128,896]{1,0:T(8,128)(2,1)} %get-tuple-element.8) | data formatting | bytes 458752
  94.0 1.1 %copy.12 = f32[128,1]{0,1:T(1,128)} copy(f32[128,1]{0,1:T(1,128)} %bitcast.11) | data formatting | bytes 1024

commit v2 on v1

v2 whole, which is shorter than its diff:
```python
import jax
import jax.numpy as jnp
from jax import lax
from jax.experimental import pallas as pl
from jax.experimental.pallas import tpu as pltpu
from jax.sharding import PartitionSpec as P

MESH = pl.DeviceIdType.MESH
BF = jnp.bfloat16
F32 = jnp.float32
NX, NC, NY, NZ = 4, 2, 4, 8
NE = NY * NZ
MOST = 8
SLOTS = NE * MOST
DZ = (0, 1, 7, 4, 2, 6, 3, 5)
CHUNKS = len(DZ)
PER = NE // CHUNKS
GROUPS = 2
CPG = CHUNKS // GROUPS
ROWS = SLOTS // GROUPS
NT = (((1,), (1,)), ((), ()))
TN = (((0,), (0,)), ((), ()))


A, B = 0, 1
SCHEDULE = tuple(("send", n) for n in range(CHUNKS)) + (
    ("own", 0), ("own", 1), ("own", 2), ("near", 0), ("near", 1), ("near", 2), ("own", 3), ("far", 0), ("near", 3),
    ("far", 1), ("far", 2), ("own", 4), ("own", 5), ("front", A, 0), ("far", 3),
    ("front", A, 1), ("front", A, 2), ("front", A, 6), ("near", 4), ("near", 5), ("own", 6), ("own", 7),
    ("front", A, 3), ("front", A, 7), ("front", A, 4), ("front", A, 5), ("middle", A),
    ("out", A, 2), ("mine", A, 2), ("out", A, 1), ("near", 6), ("paired", A, 2), ("mine", A, 1), ("far", 4),
    ("out", A, 3), ("paired", A, 1), ("near", 7), ("mine", A, 3), ("far", 5), ("out", A, 0), ("paired", A, 3),
    ("mine", A, 0), ("far", 6), ("front", B, 0), ("front", B, 1), ("front", B, 2), ("front", B, 6),
    ("front", B, 3), ("front", B, 7), ("far", 7), ("front", B, 4), ("relayed", A), ("front", B, 5), ("middle", B),
    ("route_parts",),
    ("out", B, 2), ("mine", B, 2), ("out", B, 1), ("paired", B, 2), ("mine", B, 1), ("out", B, 3), ("paired", B, 1),
    ("mine", B, 3), ("out", B, 0), ("paired", B, 3), ("mine", B, 0), ("paired", A, 0), ("finished", A),
    ("paired", B, 0), ("route_back",), ("relayed", B), ("finished", B),
)


def kernel(tok, og, ids, rw, wg_h, wu_h, wd_h, tg_out, rg_out,
           wgu, wd, packed, xg, acc, gbuf, ps, pb, own, relay, snd, fin, rets, ret,
           selbuf, rpart, rtot, rret,
           wsem, disp_r, ag_r, far_r, core_r, pair_r, rel_r, fin_r, ret_r, rp_r, rr_r, send_s):
    seq, exp = lax.axis_index("seq"), lax.axis_index("exp")
    x, c = seq // NC, seq % NC
    y, z = exp // NZ, exp % NZ
    f = tok.shape[1]

    def at_x(step, flip=0):
        return {"seq": NC * ((x + step) % NX) + (c + flip) % NC}

    def to_exp(i, dy):
        return {"exp": ((y + dy) % NY) * NZ + (z + DZ[i]) % NZ}

    def from_exp(i, dy):
        return {"exp": ((y + NY - dy) % NY) * NZ + (z + NZ - DZ[i]) % NZ}

    def copy(src, dst, ssem, rsem, dev):
        return pltpu.make_async_remote_copy(
            src_ref=src, dst_ref=dst, send_sem=ssem, recv_sem=rsem,
            device_id=dev, device_id_type=MESH)

    def got(ref, sem):
        pltpu.make_async_copy(ref, ref, sem).wait()

    wcopies = []
    for k in range(NX * NC):
        dx, flip = k // NC, k % NC
        first = pl.multiple_of((NC * ((x + NX - dx) % NX) + (c + flip) % NC) * f, 128)
        h = wg_h.shape[1]
        for n, (src, dst) in enumerate((
                (wg_h.at[pl.ds(first, f), :], wgu.at[k, :, 0:h]),
                (wu_h.at[pl.ds(first, f), :], wgu.at[k, :, h:2 * h]),
                (wd_h.at[:, pl.ds(first, f)], wd.at[k]))):
            one = pltpu.make_async_copy(src, dst, wsem.at[k, n])
            one.start()
            wcopies.append(one)

    barrier = pltpu.get_barrier_semaphore()

    for n in range(CHUNKS):
        @pl.loop(1 if n == 0 else 0, NY)
        def _(dy):
            pl.semaphore_signal(barrier, inc=1, device_id=to_exp(n, dy), device_id_type=MESH)

    for k in range(1, NX * NC):
        pl.semaphore_signal(barrier, inc=1, device_id=at_x(k // NC, k % NC), device_id_type=MESH)

    q = lax.broadcasted_iota(jnp.int32, (SLOTS, tok.shape[0]), 0)
    j = q >> 3
    i = j >> 2
    dz = jnp.zeros_like(i)
    for n in range(1, CHUNKS):
        dz = jnp.where(i == n, DZ[n], dz)
    wanted = ((y + (j & 3)) & 3) * NZ + ((z + dz) & 7)
    hot = ids[0:1, :] == wanted
    for k in range(1, ids.shape[0]):
        hot = hot | (ids[k:k + 1, :] == wanted)
    hot = jnp.where(hot, 1.0, 0.0)
    t0 = lax.broadcasted_iota(jnp.int32, (tok.shape[0], tok.shape[0]), 0)
    t1 = lax.broadcasted_iota(jnp.int32, (tok.shape[0], tok.shape[0]), 1)
    before = jnp.where(t0 < t1, 1.0, 0.0).astype(BF)
    rank = jnp.dot(hot.astype(BF), before, preferred_element_type=F32)
    sel = jnp.where(rank == (q & 7).astype(F32), hot, 0.0)
    selbuf[...] = sel
    selb = sel.astype(BF)
    for n, src in enumerate((tok, og)):
        rows = jnp.dot(selb, src[...], preferred_element_type=F32)
        rows = rows.reshape(NE, MOST, f).astype(BF)
        packed[:, :, n * f:(n + 1) * f] = rows
        xg[0, 0:1, :, n * f:(n + 1) * f] = rows[0:1]

    pl.semaphore_wait(barrier, NE - 1 + NX * NC - 1)

    def send(n):
        @pl.loop(1 if n == 0 else 0, NY)
        def _(dy):
            j = n * PER + dy
            copy(packed.at[j], xg.at[0, j], send_s.at[0], disp_r.at[n], to_exp(n, dy)).start()

    def rows_of(r):
        return pl.ds(r * PER, PER)

    def own_chunk(r):
        lo = 1 if r == 0 else r * PER
        got(xg.at[0, lo:(r + 1) * PER], disp_r.at[r])
        mine = xg.at[0, rows_of(r)]
        copy(mine, xg.at[2, rows_of(r)], send_s.at[1], ag_r.at[0, r], at_x(1)).start()
        copy(mine, xg.at[6, rows_of(r)], send_s.at[2], ag_r.at[1, r], at_x(3)).start()
        copy(mine, xg.at[1, rows_of(r)], send_s.at[3], core_r.at[0, r // CPG], at_x(0, 1)).start()

    hp = PER // 2

    def near_chunk(r):
        for n, (slot, step) in enumerate(((2, 1), (6, 3))):
            part = xg.at[slot, rows_of(r)]
            got(part, ag_r.at[n, r])
            lo = r * PER + n * hp
            copy(xg.at[slot, lo:lo + hp], xg.at[4, lo:lo + hp], send_s.at[4 + n], far_r.at[n, r], at_x(step)).start()
            copy(part, xg.at[slot + 1, rows_of(r)], send_s.at[6 + n], core_r.at[slot // 2, r // CPG], at_x(0, 1)).start()

    def far_chunk(r):
        for n in range(2):
            lo = r * PER + n * hp
            got(xg.at[4, lo:lo + hp], far_r.at[n, r])
        copy(xg.at[4, rows_of(r)], xg.at[5, rows_of(r)], send_s.at[8], core_r.at[2, r // CPG], at_x(0, 1)).start()

    h2 = wgu.shape[2]

    def front(g, k):
        if g == 0:
            for n in range(3):
                wcopies[3 * k + n].wait()
        blocks = slice(g * CPG * PER, (g + 1) * CPG * PER)
        rows = slice(g * ROWS, (g + 1) * ROWS)
        if k % 2:
            got(xg.at[k, blocks], core_r.at[k // 2, g])
        xs = xg[k, blocks, :, 0:f].reshape(ROWS, f)
        ds = xg[k, blocks, :, f:2 * f].reshape(ROWS, f)
        gu = jnp.dot(xs, wgu[k], preferred_element_type=F32)
        bg = lax.dot_general(ds, wd[k], NT, preferred_element_type=F32)
        if k == 0:
            acc[rows, 0:h2] = gu
            acc[rows, h2:] = bg
        else:
            acc[rows, 0:h2] += gu
            acc[rows, h2:] += bg

    h = h2 // 2

    def middle(g):
        rows = slice(g * ROWS, (g + 1) * ROWS)
        pre_g = acc[rows, 0:h]
        pre_u = acc[rows, h:h2]
        back = acc[rows, h2:]
        sig = 1.0 / (1.0 + jnp.exp(-pre_g))
        active = pre_g * sig
        gbuf[rows, 0:h] = (back * pre_u * sig * (1.0 + pre_g * (1.0 - sig))).astype(BF)
        gbuf[rows, h:h2] = (back * active).astype(BF)
        part = lax.dot_general(jnp.ones((8, h), F32), active * pre_u * back, NT, preferred_element_type=F32,
                               precision=lax.Precision.HIGHEST)
        rpart[0, :, rows] = part[0:1, :]

    def product(g, d, flip):
        k = ((NX - d) % NX) * NC + flip
        return lax.dot_general(gbuf[g * ROWS:(g + 1) * ROWS], wgu[k], NT, preferred_element_type=F32)

    m = ROWS // 2

    def half(g, n):
        return slice(g * ROWS + n * m, g * ROWS + (n + 1) * m)

    def out(g, d):
        rows = slice(g * ROWS, (g + 1) * ROWS)
        ps[d, rows] = product(g, d, 1).astype(BF)
        copy(ps.at[d, rows], pb.at[d, rows], send_s.at[10], pair_r.at[d, g], at_x(0, 1)).start()

    def mine(g, d):
        own[d, g * ROWS:(g + 1) * ROWS] = product(g, d, 0)

    def paired(g, d):
        rows = slice(g * ROWS, (g + 1) * ROWS)
        got(pb.at[d, rows], pair_r.at[d, g])
        if d == 0:
            own[0, rows] += pb[0, rows].astype(F32)
        elif d == 2:
            snd[0, rows] = (own[2, rows] + pb[2, rows].astype(F32)).astype(BF)
            for n, step in enumerate((1, 3)):
                copy(snd.at[0, half(g, n)], relay.at[n, g], send_s.at[11 + n], rel_r.at[n, g], at_x(step)).start()
        else:
            n = 0 if d == 1 else 1
            own[d, rows] += pb[d, rows].astype(F32)
            other = half(g, 1 - n)
            snd[1 + n, other] = own[d, other].astype(BF)
            copy(snd.at[1 + n, other], fin.at[n, other], send_s.at[13 + n], fin_r.at[n, 1 - n, g], at_x(d)).start()

    def relayed(g):
        for n, d in enumerate((1, 3)):
            got(relay.at[n, g], rel_r.at[n, g])
            this = half(g, n)
            snd[1 + n, this] = (own[d, this] + relay[n, g].astype(F32)).astype(BF)
            copy(snd.at[1 + n, this], fin.at[n, this], send_s.at[15 + n], fin_r.at[n, n, g], at_x(d)).start()

    def finished(g):
        for n in (1, 0):
            this = half(g, n)
            got(fin.at[0, this], fin_r.at[0, n, g])
            got(fin.at[1, this], fin_r.at[1, n, g])
            s = own[0, this] + fin[0, this].astype(F32) + fin[1, this].astype(F32)
            s = s.reshape(m // MOST, MOST, f).astype(BF)
            lo = (g * ROWS + n * m) // MOST
            rets[lo:lo + m // MOST] = s
            if lo == 0:
                ret[0:1] = s[0:1]
            for r in reversed(range(lo // PER, (lo + m // MOST) // PER)):
                @pl.loop(1 if r == 0 else 0, NY)
                def _(dy):
                    j = r * PER + dy
                    copy(rets.at[j], ret.at[j], send_s.at[18], ret_r, from_exp(r, dy)).start()

    def route_parts():
        for k in range(1, NX * NC):
            copy(rpart.at[0], rpart.at[k], send_s.at[9], rp_r, at_x(k // NC, k % NC)).start()

    def route_back():
        got(rpart.at[1:8], rp_r)
        total = rpart[0]
        for k in range(1, NX * NC):
            total = total + rpart[k]
        rtot[...] = total
        rret[0] = total
        for r in range(CHUNKS):
            @pl.loop(1 if r == 0 else 0, NY)
            def _(dy):
                copy(rtot, rret.at[r * PER + dy], send_s.at[17], rr_r, from_exp(r, dy)).start()

    step_of = {"own": own_chunk, "near": near_chunk, "far": far_chunk, "front": front, "middle": middle,
               "out": out, "mine": mine, "send": send, "paired": paired, "relayed": relayed, "finished": finished,
               "route_parts": route_parts, "route_back": route_back}
    for step in SCHEDULE:
        step_of[step[0]](*step[1:])

    got(rret.at[1:NE], rr_r)
    lane = lax.broadcasted_iota(jnp.int32, (NE, 1, SLOTS), 2) >> 3
    row = lax.broadcasted_iota(jnp.int32, (NE, 1, SLOTS), 0)
    by_slot = jnp.sum(jnp.where(lane == row, rret[...], 0.0), axis=0)
    by_token = jnp.dot(jnp.broadcast_to(by_slot, (8, SLOTS)), selbuf[...], preferred_element_type=F32,
                       precision=lax.Precision.HIGHEST)
    rg_out[...] = jnp.where(ids[pl.ds(seq, 1), :] < NE, by_token[0:1, :], 0.0)

    weight = jnp.sum(jnp.where(ids[...] < NE, rw[...], 0.0), axis=0, keepdims=True)
    scale = jnp.sum(selbuf[...] * weight, axis=1, keepdims=True)
    got(ret.at[1:NE], ret_r)
    rows = (ret[...].reshape(SLOTS, f).astype(F32) * scale).astype(BF)
    tg_out[...] = lax.dot_general(selbuf[...].astype(BF), rows, TN, preferred_element_type=F32).astype(BF)

    got(packed.at[1:NE], send_s.at[0])
    for n in range(1, 4):
        got(xg.at[0], send_s.at[n])
    for n in range(2):
        got(xg.at[0, 0:NE // 2], send_s.at[4 + n])
        got(xg.at[0], send_s.at[6 + n])
    got(xg.at[0], send_s.at[8])
    got(rpart.at[1:8], send_s.at[9])
    got(ps, send_s.at[10])
    for n in range(11, 17):
        got(relay.at[0], send_s.at[n])
    got(rret.at[1:NE], send_s.at[17])
    got(rets.at[1:NE], send_s.at[18])


def local(tokens, out_grad, expert_ids, route_weights, gate_proj, up_proj, down_proj):
    t, f = tokens.shape
    h = gate_proj.shape[2]
    vmem = pl.BlockSpec(memory_space=pltpu.VMEM)
    anym = pl.BlockSpec(memory_space=pl.ANY)
    dma = pltpu.SemaphoreType.DMA
    token_grad, route_grad = pl.pallas_call(
        kernel,
        out_shape=(jax.ShapeDtypeStruct((t, f), BF), jax.ShapeDtypeStruct((1, t), F32)),
        in_specs=[vmem] * 4 + [anym] * 3,
        out_specs=(vmem, vmem),
        scratch_shapes=[
            pltpu.VMEM((8, f, 2 * h), BF),
            pltpu.VMEM((8, h, f), BF),
            pltpu.VMEM((NE, MOST, 2 * f), BF),
            pltpu.VMEM((8, NE, MOST, 2 * f), BF),
            pltpu.VMEM((SLOTS, 3 * h), F32),
            pltpu.VMEM((SLOTS, 2 * h), BF),
            pltpu.VMEM((4, SLOTS, f), BF),
            pltpu.VMEM((4, SLOTS, f), BF),
            pltpu.VMEM((4, SLOTS, f), F32),
            pltpu.VMEM((2, GROUPS, ROWS // 2, f), BF),
            pltpu.VMEM((3, SLOTS, f), BF),
            pltpu.VMEM((2, SLOTS, f), BF),
            pltpu.VMEM((NE, MOST, f), BF),
            pltpu.VMEM((NE, MOST, f), BF),
            pltpu.VMEM((SLOTS, t), F32),
            pltpu.VMEM((8, 1, SLOTS), F32),
            pltpu.VMEM((1, SLOTS), F32),
            pltpu.VMEM((NE, 1, SLOTS), F32),
            dma((8, 3)), dma((CHUNKS,)), dma((2, CHUNKS)), dma((2, CHUNKS)), dma((4, GROUPS)),
            dma((4, GROUPS)), dma((2, GROUPS)), dma((2, 2, GROUPS)), dma(()), dma(()), dma(()), dma((19,)),
        ],
        compiler_params=pltpu.CompilerParams(
            collective_id=0, has_side_effects=True, vmem_limit_bytes=60 * 1024 * 1024),
        name="moe_back",
    )(tokens, out_grad, expert_ids.T, route_weights.T, gate_proj[0], up_proj[0], down_proj[0])
    return token_grad, route_grad.reshape(t, 1)


def solution(mesh):
    in_specs = (
        P("exp", "seq"),
        P("exp", "seq"),
        P("exp", None),
        P("exp", None),
        P("exp", None, "seq"),
        P("exp", None, "seq"),
        P("exp", "seq", None),
    )
    out_specs = (P("exp", "seq"), P("exp", "seq"))
    return jax.shard_map(local, mesh=mesh, in_specs=in_specs, out_specs=out_specs, check_vma=False)
```

time: 95.3 us -> 84.1 us (0.88)
  Pallas kernels: 91.7 us -> 79.8 us
    pallas_call x1, Pallas kernels: 91.7 us -> 79.8 us  [local(): pl.pallas_call(kernel, out_shape=(jax.ShapeDtypeStruct((t, f), BF), jax.S...]
where the time goes in v2:
time: 84.1 us; the launch traced here: 83.2 us
  Pallas kernels  79.8 us (95%)
  local copies, waits for them, and re-layouts  2.79 us (3%)
    pallas_call x1, Pallas kernels, local(): pl.pallas_call(kernel, out_shape=(jax.ShapeDtypeStruct((t, f), BF), jax.S...  79.8 us
    unnamed x2, local copies, waits for them, and re-layouts  2.79 us

profile of v2, /device:TPU:1, one launch (start us, length us, event | category | flops | bytes accessed | tf_op | source)
XLA Modules:
  0.0 83.2 jit_solution(11083638797964955948)
XLA Ops:
  0.6 79.8 %moe_back.1 = (bf16[128,896]{1,0:T(8,128)(2,1)}, f32[1,128]{1,0:T(1,128)}) custom-call(bf16[128,896]{1,0:T(8,128)(2,1)} %tok.1, bf16[128,896]{1,0:T(8,128)(2,1)} %og.1, s32[8,128]{1,0:T(8,128)} %bitcast.9, f32[8,128]{1,0:T(8,128)} %bitcast.10, bf16[7168,256]{1,0:T(8,128)(2,1)} %bitcast.6, bf16[7168,256]{1,0:T(8,128)(2,1)} %bitcast.7, bf16[256,7168]{1,0:T(8,128)(2,1)} %bitcast.8), custom_call_target="tpu_custom_call" | custom-call | tf_op jit(solution)/shard_map/moe_back/pallas_call | solution.py:300
  80.4 1.6 %copy.11 = bf16[128,896]{1,0:T(8,128)(2,1)} copy(bf16[128,896]{1,0:T(8,128)(2,1)} %get-tuple-element.8) | data formatting | bytes 458752
  82.1 1.1 %copy.12 = f32[128,1]{0,1:T(1,128)} copy(f32[128,1]{0,1:T(1,128)} %bitcast.11) | data formatting | bytes 1024

commit v3 on v2

--- a/solution.py
+++ b/solution.py
@@ -12,27 +12,29 @@
 NE = NY * NZ
 MOST = 8
 SLOTS = NE * MOST
-DZ = (0, 1, 7, 4, 2, 6, 3, 5)
+DZ = (0, 1, 7, 2, 6, 3, 5, 4)
+BOUND = (0, 5, 8)
 CHUNKS = len(DZ)
 PER = NE // CHUNKS
-GROUPS = 2
-CPG = CHUNKS // GROUPS
-ROWS = SLOTS // GROUPS
+GROUPS = len(BOUND) - 1
+STEP = PER * MOST
 NT = (((1,), (1,)), ((), ()))
 TN = (((0,), (0,)), ((), ()))
 
 
 A, B = 0, 1
-SCHEDULE = tuple(("send", n) for n in range(CHUNKS)) + (
-    ("own", 0), ("own", 1), ("own", 2), ("near", 0), ("near", 1), ("near", 2), ("own", 3), ("far", 0), ("near", 3),
-    ("far", 1), ("far", 2), ("own", 4), ("own", 5), ("front", A, 0), ("far", 3),
-    ("front", A, 1), ("front", A, 2), ("front", A, 6), ("near", 4), ("near", 5), ("own", 6), ("own", 7),
-    ("front", A, 3), ("front", A, 7), ("front", A, 4), ("front", A, 5), ("middle", A),
-    ("out", A, 2), ("mine", A, 2), ("out", A, 1), ("near", 6), ("paired", A, 2), ("mine", A, 1), ("far", 4),
+SCHEDULE = (
+    ("send", 0), ("signal", 0), ("known", 0), ("signal", 1), ("send", 1), ("send", 2), ("own", 0), ("known", 1),
+    ("signal", 2), ("send", 3), ("send", 4), ("known", 2), ("signal", 3), ("own", 1), ("own", 2), ("known", 3),
+    ("send", 5), ("send", 6), ("send", 7),
+    ("near", 0), ("near", 1), ("near", 2), ("own", 3), ("own", 4), ("far", 0), ("far", 1), ("far", 2),
+    ("front", A, 0), ("near", 3), ("near", 4), ("front", A, 1), ("own", 5), ("own", 6), ("far", 3), ("far", 4),
+    ("front", A, 2), ("front", A, 6), ("own", 7), ("front", A, 3), ("front", A, 7), ("front", A, 4),
+    ("front", A, 5), ("middle", A),
+    ("out", A, 2), ("mine", A, 2), ("near", 5), ("out", A, 1), ("paired", A, 2), ("near", 6), ("mine", A, 1),
     ("out", A, 3), ("paired", A, 1), ("near", 7), ("mine", A, 3), ("far", 5), ("out", A, 0), ("paired", A, 3),
-    ("mine", A, 0), ("far", 6), ("front", B, 0), ("front", B, 1), ("front", B, 2), ("front", B, 6),
-    ("front", B, 3), ("front", B, 7), ("far", 7), ("front", B, 4), ("relayed", A), ("front", B, 5), ("middle", B),
-    ("route_parts",),
+    ("mine", A, 0), ("far", 6), ("front", B, 0), ("front", B, 1), ("front", B, 2), ("front", B, 6), ("relayed", A),
+    ("front", B, 3), ("front", B, 7), ("far", 7), ("front", B, 4), ("front", B, 5), ("middle", B), ("route_parts",),
     ("out", B, 2), ("mine", B, 2), ("out", B, 1), ("paired", B, 2), ("mine", B, 1), ("out", B, 3), ("paired", B, 1),
     ("mine", B, 3), ("out", B, 0), ("paired", B, 3), ("mine", B, 0), ("paired", A, 0), ("finished", A),
     ("paired", B, 0), ("route_back",), ("relayed", B), ("finished", B),
@@ -42,7 +44,7 @@
 def kernel(tok, og, ids, rw, wg_h, wu_h, wd_h, tg_out, rg_out,
            wgu, wd, packed, xg, acc, gbuf, ps, pb, own, relay, snd, fin, rets, ret,
            selbuf, rpart, rtot, rret,
-           wsem, disp_r, ag_r, far_r, core_r, pair_r, rel_r, fin_r, ret_r, rp_r, rr_r, send_s):
+           wsem, disp_r, ag_r, far_r, core_r, pair_r, rel_r, fin_r, ret_r, rp_r, rr_r, send_s, level_s):
     seq, exp = lax.axis_index("seq"), lax.axis_index("exp")
     x, c = seq // NC, seq % NC
     y, z = exp // NZ, exp % NZ
@@ -80,11 +82,13 @@
 
     barrier = pltpu.get_barrier_semaphore()
 
-    for n in range(CHUNKS):
-        @pl.loop(1 if n == 0 else 0, NY)
-        def _(dy):
-            pl.semaphore_signal(barrier, inc=1, device_id=to_exp(n, dy), device_id_type=MESH)
-
+    def at_z(step):
+        return {"exp": y * NZ + (z + step) % NZ}
+
+    for dy in range(1, NY):
+        pl.semaphore_signal(barrier, inc=1, device_id=to_exp(0, dy), device_id_type=MESH)
+    for step in (1, NZ - 1):
+        pl.semaphore_signal(barrier, inc=1, device_id=at_z(step), device_id_type=MESH)
     for k in range(1, NX * NC):
         pl.semaphore_signal(barrier, inc=1, device_id=at_x(k // NC, k % NC), device_id_type=MESH)
 
@@ -112,13 +116,29 @@
         packed[:, :, n * f:(n + 1) * f] = rows
         xg[0, 0:1, :, n * f:(n + 1) * f] = rows[0:1]
 
-    pl.semaphore_wait(barrier, NE - 1 + NX * NC - 1)
+    pl.semaphore_wait(barrier, NY - 1 + 2 + NX * NC - 1)
 
     def send(n):
         @pl.loop(1 if n == 0 else 0, NY)
         def _(dy):
             j = n * PER + dy
             copy(packed.at[j], xg.at[0, j], send_s.at[0], disp_r.at[n], to_exp(n, dy)).start()
+
+    def signal(n):
+        for step in (1, NZ - 1):
+            pl.semaphore_signal(level_s.at[n], inc=1, device_id=at_z(step), device_id_type=MESH)
+
+    def known(n):
+        pl.semaphore_wait(level_s.at[n], 2)
+
+    def group_of(r):
+        return sum(r >= b for b in BOUND[1:-1])
+
+    def group(g):
+        return slice(BOUND[g] * STEP, BOUND[g + 1] * STEP)
+
+    def size(g):
+        return (BOUND[g + 1] - BOUND[g]) * STEP
 
     def rows_of(r):
         return pl.ds(r * PER, PER)
@@ -129,7 +149,7 @@
         mine = xg.at[0, rows_of(r)]
         copy(mine, xg.at[2, rows_of(r)], send_s.at[1], ag_r.at[0, r], at_x(1)).start()
         copy(mine, xg.at[6, rows_of(r)], send_s.at[2], ag_r.at[1, r], at_x(3)).start()
-        copy(mine, xg.at[1, rows_of(r)], send_s.at[3], core_r.at[0, r // CPG], at_x(0, 1)).start()
+        copy(mine, xg.at[1, rows_of(r)], send_s.at[3], core_r.at[0, group_of(r)], at_x(0, 1)).start()
 
     hp = PER // 2
 
@@ -139,26 +159,27 @@
             got(part, ag_r.at[n, r])
             lo = r * PER + n * hp
             copy(xg.at[slot, lo:lo + hp], xg.at[4, lo:lo + hp], send_s.at[4 + n], far_r.at[n, r], at_x(step)).start()
-            copy(part, xg.at[slot + 1, rows_of(r)], send_s.at[6 + n], core_r.at[slot // 2, r // CPG], at_x(0, 1)).start()
+            copy(part, xg.at[slot + 1, rows_of(r)], send_s.at[6 + n], core_r.at[slot // 2, group_of(r)], at_x(0, 1)).start()
 
     def far_chunk(r):
         for n in range(2):
             lo = r * PER + n * hp
             got(xg.at[4, lo:lo + hp], far_r.at[n, r])
-        copy(xg.at[4, rows_of(r)], xg.at[5, rows_of(r)], send_s.at[8], core_r.at[2, r // CPG], at_x(0, 1)).start()
+        copy(xg.at[4, rows_of(r)], xg.at[5, rows_of(r)], send_s.at[8], core_r.at[2, group_of(r)], at_x(0, 1)).start()
 
     h2 = wgu.shape[2]
 
     def front(g, k):
-        if g == 0:
-            for n in range(3):
+        for n in range(3):
+            if wcopies[3 * k + n] is not None:
                 wcopies[3 * k + n].wait()
-        blocks = slice(g * CPG * PER, (g + 1) * CPG * PER)
-        rows = slice(g * ROWS, (g + 1) * ROWS)
+                wcopies[3 * k + n] = None
+        blocks = slice(BOUND[g] * PER, BOUND[g + 1] * PER)
+        rows = group(g)
         if k % 2:
             got(xg.at[k, blocks], core_r.at[k // 2, g])
-        xs = xg[k, blocks, :, 0:f].reshape(ROWS, f)
-        ds = xg[k, blocks, :, f:2 * f].reshape(ROWS, f)
+        xs = xg[k, blocks, :, 0:f].reshape(size(g), f)
+        ds = xg[k, blocks, :, f:2 * f].reshape(size(g), f)
         gu = jnp.dot(xs, wgu[k], preferred_element_type=F32)
         bg = lax.dot_general(ds, wd[k], NT, preferred_element_type=F32)
         if k == 0:
@@ -171,7 +192,7 @@
     h = h2 // 2
 
     def middle(g):
-        rows = slice(g * ROWS, (g + 1) * ROWS)
+        rows = group(g)
         pre_g = acc[rows, 0:h]
         pre_u = acc[rows, h:h2]
         back = acc[rows, h2:]
@@ -185,30 +206,32 @@
 
     def product(g, d, flip):
         k = ((NX - d) % NX) * NC + flip
-        return lax.dot_general(gbuf[g * ROWS:(g + 1) * ROWS], wgu[k], NT, preferred_element_type=F32)
-
-    m = ROWS // 2
+        return lax.dot_general(gbuf[group(g)], wgu[k], NT, preferred_element_type=F32)
 
     def half(g, n):
-        return slice(g * ROWS + n * m, g * ROWS + (n + 1) * m)
+        first, m = BOUND[g] * STEP, size(g) // 2
+        return slice(first + n * m, first + (n + 1) * m)
+
+    def passing(g):
+        return slice(BOUND[g] * STEP // 2, BOUND[g + 1] * STEP // 2)
 
     def out(g, d):
-        rows = slice(g * ROWS, (g + 1) * ROWS)
+        rows = group(g)
         ps[d, rows] = product(g, d, 1).astype(BF)
         copy(ps.at[d, rows], pb.at[d, rows], send_s.at[10], pair_r.at[d, g], at_x(0, 1)).start()
 
     def mine(g, d):
-        own[d, g * ROWS:(g + 1) * ROWS] = product(g, d, 0)
+        own[d, group(g)] = product(g, d, 0)
 
     def paired(g, d):
-        rows = slice(g * ROWS, (g + 1) * ROWS)
+        rows = group(g)
         got(pb.at[d, rows], pair_r.at[d, g])
         if d == 0:
             own[0, rows] += pb[0, rows].astype(F32)
         elif d == 2:
             snd[0, rows] = (own[2, rows] + pb[2, rows].astype(F32)).astype(BF)
             for n, step in enumerate((1, 3)):
-                copy(snd.at[0, half(g, n)], relay.at[n, g], send_s.at[11 + n], rel_r.at[n, g], at_x(step)).start()
+                copy(snd.at[0, half(g, n)], relay.at[n, passing(g)], send_s.at[11 + n], rel_r.at[n, g], at_x(step)).start()
         else:
             n = 0 if d == 1 else 1
             own[d, rows] += pb[d, rows].astype(F32)
@@ -218,9 +241,9 @@
 
     def relayed(g):
         for n, d in enumerate((1, 3)):
-            got(relay.at[n, g], rel_r.at[n, g])
+            got(relay.at[n, passing(g)], rel_r.at[n, g])
             this = half(g, n)
-            snd[1 + n, this] = (own[d, this] + relay[n, g].astype(F32)).astype(BF)
+            snd[1 + n, this] = (own[d, this] + relay[n, passing(g)].astype(F32)).astype(BF)
             copy(snd.at[1 + n, this], fin.at[n, this], send_s.at[15 + n], fin_r.at[n, n, g], at_x(d)).start()
 
     def finished(g):
@@ -229,13 +252,17 @@
             got(fin.at[0, this], fin_r.at[0, n, g])
             got(fin.at[1, this], fin_r.at[1, n, g])
             s = own[0, this] + fin[0, this].astype(F32) + fin[1, this].astype(F32)
-            s = s.reshape(m // MOST, MOST, f).astype(BF)
-            lo = (g * ROWS + n * m) // MOST
-            rets[lo:lo + m // MOST] = s
+            lo, hi = this.start // MOST, this.stop // MOST
+            s = s.reshape(hi - lo, MOST, f).astype(BF)
+            rets[lo:hi] = s
             if lo == 0:
                 ret[0:1] = s[0:1]
-            for r in reversed(range(lo // PER, (lo + m // MOST) // PER)):
-                @pl.loop(1 if r == 0 else 0, NY)
+            for r in range(CHUNKS):
+                first, last = max(lo, r * PER, 1) - r * PER, min(hi, (r + 1) * PER) - r * PER
+                if first >= last:
+                    continue
+
+                @pl.loop(first, last)
                 def _(dy):
                     j = r * PER + dy
                     copy(rets.at[j], ret.at[j], send_s.at[18], ret_r, from_exp(r, dy)).start()
@@ -257,7 +284,7 @@
                 copy(rtot, rret.at[r * PER + dy], send_s.at[17], rr_r, from_exp(r, dy)).start()
 
     step_of = {"own": own_chunk, "near": near_chunk, "far": far_chunk, "front": front, "middle": middle,
-               "out": out, "mine": mine, "send": send, "paired": paired, "relayed": relayed, "finished": finished,
+               "out": out, "mine": mine, "send": send, "signal": signal, "known": known, "paired": paired, "relayed": relayed, "finished": finished,
                "route_parts": route_parts, "route_back": route_back}
     for step in SCHEDULE:
         step_of[step[0]](*step[1:])
@@ -312,7 +339,7 @@
             pltpu.VMEM((4, SLOTS, f), BF),
             pltpu.VMEM((4, SLOTS, f), BF),
             pltpu.VMEM((4, SLOTS, f), F32),
-            pltpu.VMEM((2, GROUPS, ROWS // 2, f), BF),
+            pltpu.VMEM((2, SLOTS // 2, f), BF),
             pltpu.VMEM((3, SLOTS, f), BF),
             pltpu.VMEM((2, SLOTS, f), BF),
             pltpu.VMEM((NE, MOST, f), BF),
@@ -323,6 +350,7 @@
             pltpu.VMEM((NE, 1, SLOTS), F32),
             dma((8, 3)), dma((CHUNKS,)), dma((2, CHUNKS)), dma((2, CHUNKS)), dma((4, GROUPS)),
             dma((4, GROUPS)), dma((2, GROUPS)), dma((2, 2, GROUPS)), dma(()), dma(()), dma(()), dma((19,)),
+            pltpu.SemaphoreType.REGULAR((4,)),
         ],
         compiler_params=pltpu.CompilerParams(
             collective_id=0, has_side_effects=True, vmem_limit_bytes=60 * 1024 * 1024),

time: 84.1 us -> 87.5 us (1.040)
  Pallas kernels: 79.8 us -> 83.9 us
    pallas_call x1, Pallas kernels: 79.8 us -> 83.9 us  [local(): pl.pallas_call(kernel, out_shape=(jax.ShapeDtypeStruct((t, f), BF), jax.S...]
where the time goes in v3:
time: 87.5 us; the launch traced here: 87.3 us
  Pallas kernels  83.9 us (96%)
  local copies, waits for them, and re-layouts  2.79 us (3%)
    pallas_call x1, Pallas kernels, local(): pl.pallas_call(kernel, out_shape=(jax.ShapeDtypeStruct((t, f), BF), jax.S...  83.9 us
    unnamed x2, local copies, waits for them, and re-layouts  2.79 us

profile of v3, /device:TPU:1, one launch (start us, length us, event | category | flops | bytes accessed | tf_op | source)
XLA Modules:
  0.0 87.3 jit_solution(7591294985595691596)
XLA Ops:
  0.6 83.9 %moe_back.1 = (bf16[128,896]{1,0:T(8,128)(2,1)}, f32[1,128]{1,0:T(1,128)}) custom-call(bf16[128,896]{1,0:T(8,128)(2,1)} %tok.1, bf16[128,896]{1,0:T(8,128)(2,1)} %og.1, s32[8,128]{1,0:T(8,128)} %bitcast.9, f32[8,128]{1,0:T(8,128)} %bitcast.10, bf16[7168,256]{1,0:T(8,128)(2,1)} %bitcast.6, bf16[7168,256]{1,0:T(8,128)(2,1)} %bitcast.7, bf16[256,7168]{1,0:T(8,128)(2,1)} %bitcast.8), custom_call_target="tpu_custom_call" | custom-call | tf_op jit(solution)/shard_map/moe_back/pallas_call | solution.py:327
  84.6 1.6 %copy.11 = bf16[128,896]{1,0:T(8,128)(2,1)} copy(bf16[128,896]{1,0:T(8,128)(2,1)} %get-tuple-element.8) | data formatting | bytes 458752
  86.2 1.1 %copy.12 = f32[128,1]{0,1:T(1,128)} copy(f32[128,1]{0,1:T(1,128)} %bitcast.11) | data formatting | bytes 1024

commit v4 on v3

--- a/solution.py
+++ b/solution.py
@@ -12,7 +12,7 @@
 NE = NY * NZ
 MOST = 8
 SLOTS = NE * MOST
-DZ = (0, 1, 7, 2, 6, 3, 5, 4)
+DZ = (0, 1, 7, 4, 2, 6, 3, 5)
 BOUND = (0, 5, 8)
 CHUNKS = len(DZ)
 PER = NE // CHUNKS
@@ -23,10 +23,8 @@
 
 
 A, B = 0, 1
-SCHEDULE = (
-    ("send", 0), ("signal", 0), ("known", 0), ("signal", 1), ("send", 1), ("send", 2), ("own", 0), ("known", 1),
-    ("signal", 2), ("send", 3), ("send", 4), ("known", 2), ("signal", 3), ("own", 1), ("own", 2), ("known", 3),
-    ("send", 5), ("send", 6), ("send", 7),
+SCHEDULE = tuple(("send", n) for n in range(CHUNKS)) + (
+    ("own", 0), ("own", 1), ("own", 2),
     ("near", 0), ("near", 1), ("near", 2), ("own", 3), ("own", 4), ("far", 0), ("far", 1), ("far", 2),
     ("front", A, 0), ("near", 3), ("near", 4), ("front", A, 1), ("own", 5), ("own", 6), ("far", 3), ("far", 4),
     ("front", A, 2), ("front", A, 6), ("own", 7), ("front", A, 3), ("front", A, 7), ("front", A, 4),
@@ -36,15 +34,15 @@
     ("mine", A, 0), ("far", 6), ("front", B, 0), ("front", B, 1), ("front", B, 2), ("front", B, 6), ("relayed", A),
     ("front", B, 3), ("front", B, 7), ("far", 7), ("front", B, 4), ("front", B, 5), ("middle", B), ("route_parts",),
     ("out", B, 2), ("mine", B, 2), ("out", B, 1), ("paired", B, 2), ("mine", B, 1), ("out", B, 3), ("paired", B, 1),
-    ("mine", B, 3), ("out", B, 0), ("paired", B, 3), ("mine", B, 0), ("paired", A, 0), ("finished", A),
-    ("paired", B, 0), ("route_back",), ("relayed", B), ("finished", B),
+    ("mine", B, 3), ("paired", A, 0), ("finished", A), ("out", B, 0), ("paired", B, 3), ("mine", B, 0),
+    ("route_back",), ("paired", B, 0), ("relayed", B), ("finished", B),
 )
 
 
 def kernel(tok, og, ids, rw, wg_h, wu_h, wd_h, tg_out, rg_out,
            wgu, wd, packed, xg, acc, gbuf, ps, pb, own, relay, snd, fin, rets, ret,
            selbuf, rpart, rtot, rret,
-           wsem, disp_r, ag_r, far_r, core_r, pair_r, rel_r, fin_r, ret_r, rp_r, rr_r, send_s, level_s):
+           wsem, disp_r, ag_r, far_r, core_r, pair_r, rel_r, fin_r, ret_r, rp_r, rr_r, send_s):
     seq, exp = lax.axis_index("seq"), lax.axis_index("exp")
     x, c = seq // NC, seq % NC
     y, z = exp // NZ, exp % NZ
@@ -66,6 +64,16 @@
 
     def got(ref, sem):
         pltpu.make_async_copy(ref, ref, sem).wait()
+
+    barrier = pltpu.get_barrier_semaphore()
+
+    for n in (3, 6, 7, 4, 5, 1, 2, 0):
+        @pl.loop(1 if n == 0 else 0, NY)
+        def _(dy):
+            pl.semaphore_signal(barrier, inc=1, device_id=to_exp(n, dy), device_id_type=MESH)
+
+    for k in range(1, NX * NC):
+        pl.semaphore_signal(barrier, inc=1, device_id=at_x(k // NC, k % NC), device_id_type=MESH)
 
     wcopies = []
     for k in range(NX * NC):
@@ -79,18 +87,6 @@
             one = pltpu.make_async_copy(src, dst, wsem.at[k, n])
             one.start()
             wcopies.append(one)
-
-    barrier = pltpu.get_barrier_semaphore()
-
-    def at_z(step):
-        return {"exp": y * NZ + (z + step) % NZ}
-
-    for dy in range(1, NY):
-        pl.semaphore_signal(barrier, inc=1, device_id=to_exp(0, dy), device_id_type=MESH)
-    for step in (1, NZ - 1):
-        pl.semaphore_signal(barrier, inc=1, device_id=at_z(step), device_id_type=MESH)
-    for k in range(1, NX * NC):
-        pl.semaphore_signal(barrier, inc=1, device_id=at_x(k // NC, k % NC), device_id_type=MESH)
 
     q = lax.broadcasted_iota(jnp.int32, (SLOTS, tok.shape[0]), 0)
     j = q >> 3
@@ -116,20 +112,13 @@
         packed[:, :, n * f:(n + 1) * f] = rows
         xg[0, 0:1, :, n * f:(n + 1) * f] = rows[0:1]
 
-    pl.semaphore_wait(barrier, NY - 1 + 2 + NX * NC - 1)
+    pl.semaphore_wait(barrier, NE - 1 + NX * NC - 1)
 
     def send(n):
         @pl.loop(1 if n == 0 else 0, NY)
         def _(dy):
             j = n * PER + dy
             copy(packed.at[j], xg.at[0, j], send_s.at[0], disp_r.at[n], to_exp(n, dy)).start()
-
-    def signal(n):
-        for step in (1, NZ - 1):
-            pl.semaphore_signal(level_s.at[n], inc=1, device_id=at_z(step), device_id_type=MESH)
-
-    def known(n):
-        pl.semaphore_wait(level_s.at[n], 2)
 
     def group_of(r):
         return sum(r >= b for b in BOUND[1:-1])
@@ -284,7 +273,7 @@
                 copy(rtot, rret.at[r * PER + dy], send_s.at[17], rr_r, from_exp(r, dy)).start()
 
     step_of = {"own": own_chunk, "near": near_chunk, "far": far_chunk, "front": front, "middle": middle,
-               "out": out, "mine": mine, "send": send, "signal": signal, "known": known, "paired": paired, "relayed": relayed, "finished": finished,
+               "out": out, "mine": mine, "send": send, "paired": paired, "relayed": relayed, "finished": finished,
                "route_parts": route_parts, "route_back": route_back}
     for step in SCHEDULE:
         step_of[step[0]](*step[1:])
@@ -350,7 +339,6 @@
             pltpu.VMEM((NE, 1, SLOTS), F32),
             dma((8, 3)), dma((CHUNKS,)), dma((2, CHUNKS)), dma((2, CHUNKS)), dma((4, GROUPS)),
             dma((4, GROUPS)), dma((2, GROUPS)), dma((2, 2, GROUPS)), dma(()), dma(()), dma(()), dma((19,)),
-            pltpu.SemaphoreType.REGULAR((4,)),
         ],
         compiler_params=pltpu.CompilerParams(
             collective_id=0, has_side_effects=True, vmem_limit_bytes=60 * 1024 * 1024),

time: 87.5 us -> 81.9 us (0.936); the launches traced: 87.3 us -> 80.5 us
  Pallas kernels: 83.9 us -> 77.1 us
    pallas_call x1, Pallas kernels: 83.9 us -> 77.1 us  [local(): pl.pallas_call(kernel, out_shape=(jax.ShapeDtypeStruct((t, f), BF), jax.S...]
where the time goes in v4:
time: 81.9 us; the launch traced here: 80.5 us
  Pallas kernels  77.1 us (94%)
  local copies, waits for them, and re-layouts  2.79 us (3%)
    pallas_call x1, Pallas kernels, local(): pl.pallas_call(kernel, out_shape=(jax.ShapeDtypeStruct((t, f), BF), jax.S...  77.1 us
    unnamed x2, local copies, waits for them, and re-layouts  2.79 us

profile of v4, /device:TPU:1, one launch (start us, length us, event | category | flops | bytes accessed | tf_op | source)
XLA Modules:
  0.0 80.5 jit_solution(1820429061889979212)
XLA Ops:
  0.6 77.1 %moe_back.1 = (bf16[128,896]{1,0:T(8,128)(2,1)}, f32[1,128]{1,0:T(1,128)}) custom-call(bf16[128,896]{1,0:T(8,128)(2,1)} %tok.1, bf16[128,896]{1,0:T(8,128)(2,1)} %og.1, s32[8,128]{1,0:T(8,128)} %bitcast.9, f32[8,128]{1,0:T(8,128)} %bitcast.10, bf16[7168,256]{1,0:T(8,128)(2,1)} %bitcast.6, bf16[7168,256]{1,0:T(8,128)(2,1)} %bitcast.7, bf16[256,7168]{1,0:T(8,128)(2,1)} %bitcast.8), custom_call_target="tpu_custom_call" | custom-call | tf_op jit(solution)/shard_map/moe_back/pallas_call | solution.py:316
  77.7 1.6 %copy.11 = bf16[128,896]{1,0:T(8,128)(2,1)} copy(bf16[128,896]{1,0:T(8,128)(2,1)} %get-tuple-element.8) | data formatting | bytes 458752
  79.3 1.1 %copy.12 = f32[128,1]{0,1:T(1,128)} copy(f32[128,1]{0,1:T(1,128)} %bitcast.11) | data formatting | bytes 1024
